TPU v7x, 512 devices: a whole 4x8x8 slice. The times are simulated.
512 devices in a mesh: src: 128 (over y, z, core), depth: 4 (over x).
Axes of the slice: x: 4, y: 8, z: 8, core: 2. Of those that a mesh axis runs over, the one named last changes fastest.
Arguments:
- incident: float32 [128, 4, 2, 4096], P('src'), may hold values from -6 to 6
- encode: int32 [128], P('src'), may hold values from 0 to 15
- freq_index: int32 [128], P('src'), may hold values from 0 to 7
- wavenum: float32 [8], replicated, may hold values from 1 to 2.8
- slowness: float32 [4, 4096], P('depth'), may hold values from -6 to 6
- probes: bfloat16 [64, 4, 4096], P(None, 'depth'), may hold values from -6 to 6
Outputs:
- sketch_basis: float32 [64, 4, 4096], P(None, 'depth', 'src')
- r_factor: float32 [64, 64], replicated
All inputs are finite; a program needn't handle non-finite values.
Results may differ from a plain program's by a relative error of at most 0.02.
Values may be sent and summed in bfloat16 or wider, within the bound.
A program may use at most 128 MiB of HBM per device.

v0:
```python
import math
import jax
import jax.numpy as jnp
from jax import lax
from jax.sharding import Mesh, PartitionSpec as P

SIDE = 64
CHIPS_Y = 8
CHIPS_Z = 8
CORES = 2
SRC_AXES = ("chip_y", "chip_z", "core")
DAMPING = 0.5
STEP_DEPTH = 1.0


def dft_tables(points, direction):
    counter = jnp.arange(points, dtype=jnp.int32)
    product = counter[:, None] * counter[None, :] % points
    angles = 2.0 * math.pi / points * product.astype(jnp.float32)
    cosine = jnp.cos(angles) / math.sqrt(points)
    sine_part = direction * jnp.sin(angles) / math.sqrt(points)
    matrix = jnp.stack(
        [jnp.stack([cosine, sine_part], axis=1), jnp.stack([-sine_part, cosine], axis=1)], axis=0
    )
    matrix = matrix.astype(jnp.bfloat16)
    total_points = points * points
    twist_index = counter[:, None] * counter[None, :] % total_points
    twist_angle = 2.0 * math.pi / total_points * twist_index.astype(jnp.float32)
    return (matrix, jnp.cos(twist_angle), direction * jnp.sin(twist_angle))


def transform(values, tables):
    matrix, twist_real, twist_imag = tables
    points = matrix.shape[1]
    leading = values.shape[:-2]
    grid_values = values.reshape((-1, 2 * points, points))
    square = matrix.reshape(2 * points, 2 * points)
    segmented = jnp.einsum("nkb,km->nbm", grid_values, square, preferred_element_type=jnp.float32)
    real_part = segmented[:, :, :points]
    imag_part = segmented[:, :, points:]
    turned = jnp.concatenate(
        [
            real_part * twist_real - imag_part * twist_imag,
            real_part * twist_imag + imag_part * twist_real,
        ],
        axis=-1,
    )
    turned = turned.astype(jnp.bfloat16).reshape((-1, points, 2, points))
    result = jnp.einsum("nbsc,sbtd->ntdc", turned, matrix, preferred_element_type=jnp.float32)
    return result.reshape(leading + (2, points * points))


def complex_times(first, second):
    real_part = first[..., 0, :] * second[..., 0, :] - first[..., 1, :] * second[..., 1, :]
    imag_part = first[..., 0, :] * second[..., 1, :] + first[..., 1, :] * second[..., 0, :]
    return jnp.stack([real_part, imag_part], axis=-2)


def conjugate(values):
    return jnp.stack([values[..., 0, :], -values[..., 1, :]], axis=-2)


def propagate(values, spectrum, forward, inverse):
    moved_on = transform(values.astype(jnp.bfloat16), forward)
    return transform(complex_times(moved_on, spectrum).astype(jnp.bfloat16), inverse)


def propagator(wave_nums, points_all):
    counter = jnp.arange(points_all, dtype=jnp.int32)
    folded = jnp.where(counter < points_all // 2, counter, counter - points_all).astype(jnp.float32)
    lateral = 2.0 * math.pi / points_all * folded
    excess = wave_nums[:, None] ** 2 - lateral[None, :] ** 2
    upward = jnp.sqrt(jnp.maximum(excess, 0.0)) * STEP_DEPTH
    damped = jnp.sqrt(jnp.maximum(-excess, 0.0)) * STEP_DEPTH
    real_part = jnp.where(excess > 0, jnp.cos(upward), jnp.exp(-damped))
    imag_part = jnp.where(excess > 0, jnp.sin(upward), jnp.zeros_like(upward))
    return jnp.stack([real_part, imag_part], axis=1)


def screens(wave_nums, slowness):
    phase = wave_nums[:, None, None] * STEP_DEPTH * slowness[None]
    return jnp.stack([jnp.cos(phase), jnp.sin(phase)], axis=2)


def encoded_sources(incident, encode, sources):
    shifts = jnp.arange(sources, dtype=jnp.int32)
    bit_set = encode[:, None] >> shifts[None, :] & 1
    signs_all = (1 - 2 * bit_set).astype(jnp.float32)
    return jnp.sum(signs_all[:, :, None, None] * incident, axis=1)


def lookup_waves(freq_index, wavenum, table_size):
    onehot_rows = (freq_index[:, None] == jnp.arange(table_size, dtype=jnp.int32)[None, :]).astype(
        jnp.float32
    )
    return jnp.sum(onehot_rows * wavenum[None, :], axis=1)


def shards(incident, encode, freq_index, wavenum, slowness, probes):
    points_all = SIDE * SIDE
    forward = dft_tables(SIDE, -1.0)
    inverse = dft_tables(SIDE, 1.0)
    group_count = incident.shape[0]
    probe_count = probes.shape[0]
    src_count = lax.axis_size(SRC_AXES)
    depth_count = lax.axis_size("depth")
    slowness_all = lax.all_gather(slowness, "depth", axis=0, tiled=True)
    plane_count = slowness_all.shape[0]
    probe_mine = lax.all_to_all(probes, "depth", 0, 1, tiled=True).astype(jnp.float32)
    sources = encoded_sources(incident, encode, incident.shape[1])
    wave_nums = lookup_waves(freq_index, wavenum, wavenum.shape[0])
    spectra = propagator(wave_nums, points_all)
    spectra_back = conjugate(spectra)
    plane_screens = screens(wave_nums, slowness_all)
    born_scale = wave_nums * STEP_DEPTH
    fields = []
    current = sources
    for plane in range(plane_count):
        current = complex_times(
            plane_screens[:, plane], propagate(current, spectra, forward, inverse)
        )
        fields.append(current)

    def born(plane):
        scaled = born_scale[:, None, None] * probe_mine[None, :, plane]
        background = fields[plane]
        return jnp.stack(
            [-scaled * background[:, None, 1], scaled * background[:, None, 0]], axis=2
        )

    tangent = born(0)
    for plane in range(1, plane_count):
        moved_on = complex_times(
            plane_screens[:, plane][:, None], propagate(tangent, spectra[:, None], forward, inverse)
        )
        tangent = moved_on + born(plane)
    adjoint = tangent
    pieces = [None] * plane_count
    for plane in reversed(range(plane_count)):
        background = fields[plane]
        product_terms = born_scale[:, None, None] * (
            background[:, None, 0] * adjoint[:, :, 1] - background[:, None, 1] * adjoint[:, :, 0]
        )
        pieces[plane] = jnp.sum(product_terms, axis=0)
        if plane > 0:
            turned_back = complex_times(conjugate(plane_screens[:, plane])[:, None], adjoint)
            adjoint = propagate(turned_back, spectra_back[:, None], forward, inverse)
    sketch_part = jnp.stack(pieces, axis=1)
    rows, planes = (sketch_part.shape[0], sketch_part.shape[1])
    by_axes = sketch_part.reshape(rows, planes, CHIPS_Y, CHIPS_Z, CORES, -1)
    by_axes = jnp.transpose(by_axes, (4, 3, 2, 0, 1, 5))
    summed = lax.psum_scatter(by_axes, "core", scatter_dimension=0)
    summed = lax.psum_scatter(summed, "chip_z", scatter_dimension=0)
    summed = lax.psum_scatter(summed, "chip_y", scatter_dimension=0)
    summed = lax.all_gather(summed, "depth", axis=0, tiled=True)
    slab_width = summed.shape[2]
    src_index = lax.axis_index(SRC_AXES)
    local_probes = lax.dynamic_slice_in_dim(probes, src_index * slab_width, slab_width, 2)
    local_probes = lax.all_gather(local_probes, "depth", axis=1, tiled=True).astype(jnp.float32)
    sketch_all = summed / (group_count * src_count) + DAMPING * local_probes
    flattened_all = sketch_all.reshape(probe_count, -1)
    row_total = flattened_all.shape[1] * src_count
    gram_local = (
        jnp.dot(flattened_all, flattened_all.T, precision=lax.Precision.HIGHEST) / row_total
    )
    gram_matrix = lax.psum(gram_local, "core")
    gram_matrix = lax.psum(gram_matrix, "chip_z")
    gram_matrix = lax.psum(gram_matrix, "chip_y")
    sketch = lax.dynamic_slice_in_dim(sketch_all, lax.axis_index("depth"), 1, 1)
    local_planes = 1
    flattened = sketch.reshape(probe_count, local_planes * slab_width)
    lower_factor = jnp.linalg.cholesky(gram_matrix)
    identity = jnp.eye(probe_count, dtype=jnp.float32)
    inverse_lower = lax.linalg.triangular_solve(lower_factor, identity, left_side=True, lower=True)
    sketch_basis = jnp.dot(inverse_lower, flattened, precision=lax.Precision.HIGHEST).reshape(
        probe_count, local_planes, slab_width
    )
    return (sketch_basis, lower_factor.T)


def solution(mesh):
    src_size, depth_size = mesh.devices.shape
    cut = mesh.devices.reshape(CHIPS_Y, CHIPS_Z, CORES, depth_size)
    fine = Mesh(cut, SRC_AXES + ("depth",))
    in_specs = (
        P(SRC_AXES, None, None, None),
        P(SRC_AXES),
        P(SRC_AXES),
        P(),
        P("depth", None),
        P(None, "depth", None),
    )
    out_specs = (P(None, "depth", SRC_AXES), P())
    return jax.shard_map(shards, mesh=fine, in_specs=in_specs, out_specs=out_specs, check_vma=False)
```

profile of v0, /device:TPU:2, one launch (start us, length us, event | category | flops | bytes accessed | tf_op | source)
XLA Modules:
  0.0 331.6 jit_solution(9152057225294256255)
XLA Ops:
  7.7 2.0 reduce.49
  9.7 1.2 reshape.3022
  10.9 9.3 %all-to-all-start = ((bf16[4,2,32768]{2,1,0:T(2,128)(2,1)}), bf16[4,2,32768]{2,1,0:T(2,128)(2,1)S(1)}, u32[]{:S(2)}, u32[]{:S(2)}) async-start(bf16[4,2,32768]{2,1,0:T(2,128)(2,1)} %reshape.3022), calls=%async_computation | async-start | bytes 1048576 | tf_op jit(solution)/shard_map/all_to_all | solution.py:109
  21.4 1.3 fusion.124
  25.0 12.6 %all-gather.1 = f32[4,1,4096]{2,1,0:T(1,128)S(1)} all-gather(f32[1,1,4096]{2,1,0:T(1,128)} %bitcast.531), channel_id=1, replica_groups=mesh['chip_y'=8,'chip_z'=8,'core'=2,'depth'=4] {'depth'}, dimensions={0}, use_global_device_ids=true | all-gather | bytes 81920 | tf_op jit(solution)/shard_map/all_gather | solution.py:107
  37.7 2.5 cosine_bitcast_fusion
  55.3 1.2 fusion.134
  66.3 1.7 multiply_bitcast_fusion.1
  86.7 0.9 subtract_convert_fusion.15
  91.6 0.8 subtract_convert_fusion.13
  96.4 0.9 squeeze.29
  97.3 1.9 squeeze.28
  99.2 2.1 squeeze.31
  101.3 2.8 squeeze.30
  104.1 1.9 squeeze.33
  106.0 1.9 squeeze.32
  108.0 1.8 squeeze.35
  109.8 1.9 squeeze.34
  111.8 2.3 subtract_multiply_fusion.3
  114.1 2.1 subtract_multiply_fusion.2
  117.8 2.2 maximum_bitcast_fusion
  120.1 4.4 %copy.305 = f32[2,8,8,16,4,32]{5,3,4,2,1,0:T(8,128)} copy(f32[2,8,8,16,4,32]{5,0,1,2,3,4:T(2,128)S(1)} %maximum_bitcast_fusion) | data formatting | bytes 2097152 | tf_op jit(solution)/shard_map/transpose | solution.py:151
  124.5 20.2 %reduce-scatter.4.cloned.1.call-done = f32[1,8,8,16,4,32]{5,3,4,2,1,0:T(8,128)} async-done(((f32[2,8,8,16,4,32]{5,3,4,2,1,0:T(8,128)}), f32[1,8,8,16,4,32]{5,3,4,2,1,0:T(8,128)}) %reduce-scatter.4.cloned.1.call-update) | async-done | bytes 524304 | tf_op jit(solution)/shard_map/reduce_scatter | solution.py:152
  144.8 49.8 %reduce-scatter.6.cloned.1.call-done = f32[1,8,16,4,32]{4,2,3,1,0:T(8,128)} async-done(((f32[8,8,16,4,32]{4,2,3,1,0:T(8,128)}), f32[1,8,16,4,32]{4,2,3,1,0:T(8,128)}) %reduce-scatter.6.cloned.1.call-update) | async-done | bytes 65552 | tf_op jit(solution)/shard_map/reduce_scatter | solution.py:153
  195.5 12.2 %all_gather.11 = bf16[64,4,32]{0,2,1:T(8,128)(2,1)S(1)} all-gather(bf16[64,1,32]{0,2,1:T(8,128)(2,1)S(1)} %copy.373), channel_id=1, replica_groups=mesh['chip_y'=8,'chip_z'=8,'core'=2,'depth'=4] {'depth'}, dimensions={1}, use_global_device_ids=true | all-gather | bytes 20480 | tf_op jit(solution)/shard_map/all_gather | solution.py:159
  207.7 27.2 %reduce-scatter.8.cloned.1.call-done = f32[1,16,4,32]{3,1,2,0:T(8,128)} async-done(((f32[8,16,4,32]{3,1,2,0:T(8,128)}), f32[1,16,4,32]{3,1,2,0:T(8,128)}) %reduce-scatter.8.cloned.1.call-update) | async-done | bytes 8208 | tf_op jit(solution)/shard_map/reduce_scatter | solution.py:154
  235.7 12.0 %all-gather = f32[1,64,4,32]{3,2,0,1:T(4,128)S(1)} all-gather(f32[1,16,4,32]{3,2,0,1:T(4,128)S(1)} %copy.306), channel_id=2, replica_groups=mesh['chip_y'=8,'chip_z'=8,'core'=2,'depth'=4] {'depth'}, dimensions={1}, use_global_device_ids=true | all-gather | bytes 40960 | tf_op jit(solution)/shard_map/all_gather | solution.py:155
  248.1 3.4 %psum.21 = f32[64,64]{0,1:T(8,128)S(1)} all-reduce(f32[64,64]{0,1:T(8,128)S(1)} %fusion), channel_id=1, replica_groups=mesh['chip_y'=8,'chip_z'=8,'core'=2,'depth'=4] {'core'}, use_global_device_ids=true, to_apply=%region_5.6 | all-reduce | flops 4096 | bytes 32768 | tf_op jit(solution)/shard_map/psum | solution.py:166
  251.5 30.9 %psum.22 = f32[64,64]{0,1:T(8,128)S(1)} all-reduce(f32[64,64]{0,1:T(8,128)S(1)} %psum.21), channel_id=1, replica_groups=mesh['chip_y'=8,'chip_z'=8,'core'=2,'depth'=4] {'chip_z'}, use_global_device_ids=true, to_apply=%region_6.7 | all-reduce | flops 4096 | bytes 32768 | tf_op jit(solution)/shard_map/psum | solution.py:167
  282.4 28.3 %psum.23 = f32[64,64]{0,1:T(8,128)S(1)} all-reduce(f32[64,64]{0,1:T(8,128)S(1)} %psum.22), channel_id=1, replica_groups=mesh['chip_y'=8,'chip_z'=8,'core'=2,'depth'=4] {'chip_y'}, use_global_device_ids=true, to_apply=%region_7.8 | all-reduce | flops 4096 | bytes 32768 | tf_op jit(solution)/shard_map/psum | solution.py:168
  310.8 5.8 %cholesky.17 = f32[64,64]{1,0:T(8,128)S(1)} custom-call(f32[64,64]{1,0:T(8,128)S(1)} %fusion.80), custom_call_target="Cholesky" | custom-call | tf_op jit(solution)/shard_map/jit(cholesky)/cholesky | solution.py:172
  318.0 4.9 %custom-call.6 = f32[1,64,64]{1,2,0:T(8,128)S(1)} custom-call(f32[1,64,64]{2,1,0:T(8,128)S(1)} %get-tuple-element.115), custom_call_target="InvertDiagBlocksLowerTriangular" | custom-call | tf_op jit(solution)/shard_map/triangular_solve | solution.py:174
  (286 shorter events, 58.8 us)
Async XLA Ops:
  7.2 34.7 %copy-start.16 = (f32[1,4,2,4096]{3,2,1,0:T(2,128)S(1)}, f32[1,4,2,4096]{3,2,1,0:T(2,128)}, u32[]{:S(2)}) copy-start(f32[1,4,2,4096]{3,2,1,0:T(2,128)} %param.6) | copy-start | bytes 393220
  10.9 54.0 %all-to-all-start = ((bf16[4,2,32768]{2,1,0:T(2,128)(2,1)}), bf16[4,2,32768]{2,1,0:T(2,128)(2,1)S(1)}, u32[]{:S(2)}, u32[]{:S(2)}) async-start(bf16[4,2,32768]{2,1,0:T(2,128)(2,1)} %reshape.3022), calls=%async_computation | async-start | bytes 1048576 | tf_op jit(solution)/shard_map/all_to_all | solution.py:109
  20.2 124.5 %reduce-scatter.4.cloned.1.call-start = ((), (), s32[]{:S(2)}) async-start(), calls=%async_computation.4 | async-start | bytes 6291456 | tf_op jit(solution)/shard_map/reduce_scatter | solution.py:152
  45.9 20.3 %copy-start.14 = (f32[1,1,4096]{2,1,0:T(1,128)}, f32[1,1,4096]{2,1,0:T(1,128)S(1)}, u32[]{:S(2)}) copy-start(f32[1,1,4096]{2,1,0:T(1,128)S(1)} %get-tuple-element.15) | copy-start | bytes 49156
  46.0 20.3 %copy-start.15 = (f32[1,1,4096]{2,1,0:T(1,128)}, f32[1,1,4096]{2,1,0:T(1,128)S(1)}, u32[]{:S(2)}) copy-start(f32[1,1,4096]{2,1,0:T(1,128)S(1)} %get-tuple-element.111) | copy-start | bytes 49156
  49.3 17.0 %copy-start.10 = (f32[1,1,4096]{2,1,0:T(1,128)}, f32[1,1,4096]{2,1,0:T(1,128)S(1)}, u32[]{:S(2)}) copy-start(f32[1,1,4096]{2,1,0:T(1,128)S(1)} %get-tuple-element.19) | copy-start | bytes 49156
  49.3 17.0 %copy-start.11 = (f32[1,1,4096]{2,1,0:T(1,128)}, f32[1,1,4096]{2,1,0:T(1,128)S(1)}, u32[]{:S(2)}) copy-start(f32[1,1,4096]{2,1,0:T(1,128)S(1)} %get-tuple-element.107) | copy-start | bytes 49156
  52.6 13.7 %copy-start.12 = (f32[1,1,4096]{2,1,0:T(1,128)}, f32[1,1,4096]{2,1,0:T(1,128)S(1)}, u32[]{:S(2)}) copy-start(f32[1,1,4096]{2,1,0:T(1,128)S(1)} %get-tuple-element.23) | copy-start | bytes 49156
  52.6 13.7 %copy-start.13 = (f32[1,1,4096]{2,1,0:T(1,128)}, f32[1,1,4096]{2,1,0:T(1,128)S(1)}, u32[]{:S(2)}) copy-start(f32[1,1,4096]{2,1,0:T(1,128)S(1)} %get-tuple-element.105) | copy-start | bytes 49156
  79.5 2.1 copy-start.17
  79.5 2.1 copy-start.18
  80.3 1.5 copy-start.23
  80.3 1.5 copy-start.24
  82.5 2.1 copy-start.9
  84.7 2.0 copy-start.21
  84.7 2.0 copy-start.22
  89.5 2.0 copy-start.19
  89.5 2.0 copy-start.20
  96.4 7.8 %copy-start.4 = (f32[1,16,1,4096]{3,1,2,0:T(8,128)S(1)}, f32[1,16,1,4096]{3,1,2,0:T(8,128)}, u32[]{:S(2)}) copy-start(f32[1,16,1,4096]{3,1,2,0:T(8,128)} %get-tuple-element.89) | copy-start | bytes 786436
  96.4 9.7 %copy-start.3 = (f32[1,16,1,4096]{3,1,2,0:T(8,128)S(1)}, f32[1,16,1,4096]{3,1,2,0:T(8,128)}, u32[]{:S(2)}) copy-start(f32[1,16,1,4096]{3,1,2,0:T(8,128)} %get-tuple-element.88) | copy-start | bytes 786436
  99.2 12.5 %copy-start.5 = (f32[8,8,2,32]{3,2,1,0:T(2,128)S(1)}, f32[8,8,2,32]{3,2,1,0:T(2,128)}, u32[]{:S(2)}) copy-start(f32[8,8,2,32]{3,2,1,0:T(2,128)} %mul.2738) | copy-start | bytes 49156
  111.7 4.4 %copy-start = (f32[16,1,8,8,2,32]{5,4,3,2,0,1:T(2,128)S(1)}, f32[16,1,8,8,2,32]{5,4,3,2,0,1:T(2,128)}, u32[]{:S(2)}) copy-start(f32[16,1,8,8,2,32]{5,4,3,2,0,1:T(2,128)} %squeeze.33) | copy-start | bytes 786436
  111.7 4.5 %copy-start.2 = (f32[16,1,8,8,2,32]{5,4,3,2,0,1:T(2,128)S(1)}, f32[16,1,8,8,2,32]{5,4,3,2,0,1:T(2,128)}, u32[]{:S(2)}) copy-start(f32[16,1,8,8,2,32]{5,4,3,2,0,1:T(2,128)} %squeeze.32) | copy-start | bytes 786436
  111.7 4.5 %copy-start.6 = (f32[8,8,2,32]{3,2,1,0:T(2,128)S(1)}, f32[8,8,2,32]{3,2,1,0:T(2,128)}, u32[]{:S(2)}) copy-start(f32[8,8,2,32]{3,2,1,0:T(2,128)} %mul.2752) | copy-start | bytes 49156
  111.7 4.5 %copy-start.8 = (f32[8,8,2,32]{3,2,1,0:T(2,128)S(1)}, f32[8,8,2,32]{3,2,1,0:T(2,128)}, u32[]{:S(2)}) copy-start(f32[8,8,2,32]{3,2,1,0:T(2,128)} %mul.2749) | copy-start | bytes 49156
  111.7 5.3 %copy-start.1 = (f32[16,1,8,8,2,32]{5,4,3,2,0,1:T(2,128)S(1)}, f32[16,1,8,8,2,32]{5,4,3,2,0,1:T(2,128)}, u32[]{:S(2)}) copy-start(f32[16,1,8,8,2,32]{5,4,3,2,0,1:T(2,128)} %squeeze.34) | copy-start | bytes 786436
  111.7 5.3 %copy-start.7 = (f32[8,8,2,32]{3,2,1,0:T(2,128)S(1)}, f32[8,8,2,32]{3,2,1,0:T(2,128)}, u32[]{:S(2)}) copy-start(f32[8,8,2,32]{3,2,1,0:T(2,128)} %mul.2756) | copy-start | bytes 49156
  124.5 70.1 %reduce-scatter.6.cloned.1.call-start = ((), (), s32[]{:S(2)}) async-start(), calls=%async_computation.5 | async-start | bytes 2359296 | tf_op jit(solution)/shard_map/reduce_scatter | solution.py:153
  144.7 90.2 %reduce-scatter.8.cloned.1.call-start = ((), (), s32[]{:S(2)}) async-start(), calls=%async_computation.6 | async-start | bytes 294912 | tf_op jit(solution)/shard_map/reduce_scatter | solution.py:154
Sparse Core Ops, SparseCore 0:
  124.6 20.0 reduce-scatter.3
  147.8 46.7 reduce-scatter.5
  197.6 37.2 reduce-scatter.7
where the time goes:
time: 335 us; the launch traced here: 332 us
  blocking collectives  99.4 us (30%)
  waiting for transfers between devices  97.2 us (29%)
  local copies, waits for them, and re-layouts  49 us (15%)
  other arithmetic  46.4 us (14%)
  between operations  18.1 us (5%)
  matrix products  12 us (4%)
  starting transfers between devices  9.43 us (3%)
    reduce_scatter x1, waiting for transfers between devices, shards(): summed = lax.psum_scatter(summed, 'chip_z', scatter_dimension=0)  49.8 us
    psum x1, blocking collectives, shards(): gram_matrix = lax.psum(gram_matrix, 'chip_z')  30.9 us
    psum x1, blocking collectives, shards(): gram_matrix = lax.psum(gram_matrix, 'chip_y')  28.3 us
    reduce_scatter x1, waiting for transfers between devices, shards(): summed = lax.psum_scatter(summed, 'chip_y', scatter_dimension=0)  27.2 us
    reduce_scatter x1, waiting for transfers between devices, shards(): summed = lax.psum_scatter(by_axes, 'core', scatter_dimension=0)  20.2 us
    all_gather x1, blocking collectives, shards(): slowness_all = lax.all_gather(slowness, 'depth', axis=0, tiled=True)  12.6 us
    all_gather x1, blocking collectives, shards(): lax.all_gather(local_probes, 'depth', axis=1, tiled=True)  12.2 us
    all_gather x1, blocking collectives, shards(): summed = lax.all_gather(summed, 'depth', axis=0, tiled=True)  12 us
  transfers between devices with their start and end apart: 4, of which 3 were waited for; matrix products, arithmetic and copies ran while one was open for 9% of the time, Pallas kernels for 0%

commit v1 on v0

--- a/solution.py
+++ b/solution.py
@@ -106,7 +106,10 @@
     depth_count = lax.axis_size("depth")
     slowness_all = lax.all_gather(slowness, "depth", axis=0, tiled=True)
     plane_count = slowness_all.shape[0]
-    probe_mine = lax.all_to_all(probes, "depth", 0, 1, tiled=True).astype(jnp.float32)
+    probe_mine = jnp.concatenate(
+        lax.all_to_all(jnp.stack(jnp.split(probes, lax.axis_size("depth"), axis=0)), "depth", 0, 0),
+        axis=1,
+    ).astype(jnp.float32)
     sources = encoded_sources(incident, encode, incident.shape[1])
     wave_nums = lookup_waves(freq_index, wavenum, wavenum.shape[0])
     spectra = propagator(wave_nums, points_all)

time: 335 us -> 331 us (0.988)
    another operation x30 -> x31, other arithmetic: 7.19 us -> 8.04 us
where the time goes in v1:
time: 331 us; the launch traced here: 327 us
  blocking collectives  98.5 us (30%)
  waiting for transfers between devices  97.6 us (29%)
  local copies, waits for them, and re-layouts  47 us (14%)
  other arithmetic  44.6 us (13%)
  between operations  17.7 us (5%)
  matrix products  12 us (4%)
  starting transfers between devices  9.43 us (3%)
    reduce_scatter x1, waiting for transfers between devices, shards(): summed = lax.psum_scatter(summed, 'chip_z', scatter_dimension=0)  50.1 us
    psum x1, blocking collectives, shards(): gram_matrix = lax.psum(gram_matrix, 'chip_z')  30.8 us
    psum x1, blocking collectives, shards(): gram_matrix = lax.psum(gram_matrix, 'chip_y')  28.4 us
    reduce_scatter x1, waiting for transfers between devices, shards(): summed = lax.psum_scatter(summed, 'chip_y', scatter_dimension=0)  27.3 us
    reduce_scatter x1, waiting for transfers between devices, shards(): summed = lax.psum_scatter(by_axes, 'core', scatter_dimension=0)  20.2 us
    all_gather x1, blocking collectives, shards(): slowness_all = lax.all_gather(slowness, 'depth', axis=0, tiled=True)  12.1 us
    all_gather x1, blocking collectives, shards(): summed = lax.all_gather(summed, 'depth', axis=0, tiled=True)  12 us
    all_gather x1, blocking collectives, shards(): lax.all_gather(local_probes, 'depth', axis=1, tiled=True)  11.8 us
  transfers between devices with their start and end apart: 4, of which 3 were waited for; matrix products, arithmetic and copies ran while one was open for 9% of the time, Pallas kernels for 0%

profile of v1, /device:TPU:2, one launch (start us, length us, event | category | flops | bytes accessed | tf_op | source)
XLA Modules:
  0.0 327.0 jit_solution(7855665159407990239)
XLA Ops:
  7.2 1.2 slice_bitcast_fusion.3
  8.3 0.9 pad_maximum_fusion
  9.2 9.3 %all-to-all-start = ((bf16[4,16,1,4096]{3,1,2,0:T(8,128)(2,1)}), bf16[4,16,1,4096]{3,1,2,0:T(8,128)(2,1)S(1)}, u32[]{:S(2)}, u32[]{:S(2)}) async-start(bf16[4,16,1,4096]{3,1,2,0:T(8,128)(2,1)} %pad_maximum_fusion), calls=%async_computation | async-start | bytes 1048576 | tf_op jit(solution)/shard_map/all_to_all | solution.py:110
  19.7 1.3 fusion.124
  23.2 12.1 %all-gather.1 = f32[4,1,4096]{2,1,0:T(1,128)S(1)} all-gather(f32[1,1,4096]{2,1,0:T(1,128)} %bitcast.534), channel_id=1, replica_groups=mesh['chip_y'=8,'chip_z'=8,'core'=2,'depth'=4] {'depth'}, dimensions={0}, use_global_device_ids=true | all-gather | bytes 81920 | tf_op jit(solution)/shard_map/all_gather | solution.py:107
  35.3 3.0 cosine_bitcast_fusion
  67.5 0.8 multiply_subtract_fusion.2
  82.3 0.9 subtract_convert_fusion.15
  87.3 0.8 subtract_convert_fusion.13
  92.2 0.9 squeeze.29
  93.1 1.9 squeeze.28
  95.0 1.9 squeeze.31
  96.8 2.8 squeeze.30
  99.7 1.9 squeeze.33
  101.5 1.9 squeeze.32
  103.5 1.8 squeeze.35
  105.3 1.9 squeeze.34
  107.3 2.6 subtract_multiply_fusion.3
  109.9 2.0 subtract_multiply_fusion.2
  113.4 2.2 maximum_bitcast_fusion
  115.7 4.4 %copy.301 = f32[2,8,8,16,4,32]{5,3,4,2,1,0:T(8,128)} copy(f32[2,8,8,16,4,32]{5,0,1,2,3,4:T(2,128)S(1)} %maximum_bitcast_fusion) | data formatting | bytes 2097152 | tf_op jit(solution)/shard_map/transpose | solution.py:154
  120.1 20.2 %reduce-scatter.4.cloned.1.call-done = f32[1,8,8,16,4,32]{5,3,4,2,1,0:T(8,128)} async-done(((f32[2,8,8,16,4,32]{5,3,4,2,1,0:T(8,128)}), f32[1,8,8,16,4,32]{5,3,4,2,1,0:T(8,128)}) %reduce-scatter.4.cloned.1.call-update) | async-done | bytes 524304 | tf_op jit(solution)/shard_map/reduce_scatter | solution.py:155
  140.4 50.1 %reduce-scatter.6.cloned.1.call-done = f32[1,8,16,4,32]{4,2,3,1,0:T(8,128)} async-done(((f32[8,8,16,4,32]{4,2,3,1,0:T(8,128)}), f32[1,8,16,4,32]{4,2,3,1,0:T(8,128)}) %reduce-scatter.6.cloned.1.call-update) | async-done | bytes 65552 | tf_op jit(solution)/shard_map/reduce_scatter | solution.py:156
  190.5 0.8 constant_dynamic-slice_fusion
  191.4 11.8 %all_gather.11 = bf16[64,4,32]{0,2,1:T(8,128)(2,1)S(1)} all-gather(bf16[64,1,32]{0,2,1:T(8,128)(2,1)S(1)} %copy.369), channel_id=1, replica_groups=mesh['chip_y'=8,'chip_z'=8,'core'=2,'depth'=4] {'depth'}, dimensions={1}, use_global_device_ids=true | all-gather | bytes 20480 | tf_op jit(solution)/shard_map/all_gather | solution.py:162
  203.2 27.3 %reduce-scatter.8.cloned.1.call-done = f32[1,16,4,32]{3,1,2,0:T(8,128)} async-done(((f32[8,16,4,32]{3,1,2,0:T(8,128)}), f32[1,16,4,32]{3,1,2,0:T(8,128)}) %reduce-scatter.8.cloned.1.call-update) | async-done | bytes 8208 | tf_op jit(solution)/shard_map/reduce_scatter | solution.py:157
  231.3 12.0 %all-gather = f32[1,64,4,32]{3,2,0,1:T(4,128)S(1)} all-gather(f32[1,16,4,32]{3,2,0,1:T(4,128)S(1)} %copy.302), channel_id=2, replica_groups=mesh['chip_y'=8,'chip_z'=8,'core'=2,'depth'=4] {'depth'}, dimensions={1}, use_global_device_ids=true | all-gather | bytes 40960 | tf_op jit(solution)/shard_map/all_gather | solution.py:158
  243.7 3.4 %psum.21 = f32[64,64]{0,1:T(8,128)S(1)} all-reduce(f32[64,64]{0,1:T(8,128)S(1)} %fusion), channel_id=1, replica_groups=mesh['chip_y'=8,'chip_z'=8,'core'=2,'depth'=4] {'core'}, use_global_device_ids=true, to_apply=%region_5.6 | all-reduce | flops 4096 | bytes 32768 | tf_op jit(solution)/shard_map/psum | solution.py:169
  247.1 30.8 %psum.22 = f32[64,64]{0,1:T(8,128)S(1)} all-reduce(f32[64,64]{0,1:T(8,128)S(1)} %psum.21), channel_id=1, replica_groups=mesh['chip_y'=8,'chip_z'=8,'core'=2,'depth'=4] {'chip_z'}, use_global_device_ids=true, to_apply=%region_6.7 | all-reduce | flops 4096 | bytes 32768 | tf_op jit(solution)/shard_map/psum | solution.py:170
  277.9 28.4 %psum.23 = f32[64,64]{0,1:T(8,128)S(1)} all-reduce(f32[64,64]{0,1:T(8,128)S(1)} %psum.22), channel_id=1, replica_groups=mesh['chip_y'=8,'chip_z'=8,'core'=2,'depth'=4] {'chip_y'}, use_global_device_ids=true, to_apply=%region_7.8 | all-reduce | flops 4096 | bytes 32768 | tf_op jit(solution)/shard_map/psum | solution.py:171
  306.4 5.8 %cholesky.17 = f32[64,64]{1,0:T(8,128)S(1)} custom-call(f32[64,64]{1,0:T(8,128)S(1)} %fusion.80), custom_call_target="Cholesky" | custom-call | tf_op jit(solution)/shard_map/jit(cholesky)/cholesky | solution.py:175
  313.6 4.9 %custom-call.6 = f32[1,64,64]{1,2,0:T(8,128)S(1)} custom-call(f32[1,64,64]{2,1,0:T(8,128)S(1)} %get-tuple-element.119), custom_call_target="InvertDiagBlocksLowerTriangular" | custom-call | tf_op jit(solution)/shard_map/triangular_solve | solution.py:177
  (272 shorter events, 57.3 us)
Async XLA Ops:
  7.2 32.8 %copy-start.10 = (f32[1,4,2,4096]{3,2,1,0:T(2,128)S(1)}, f32[1,4,2,4096]{3,2,1,0:T(2,128)}, u32[]{:S(2)}) copy-start(f32[1,4,2,4096]{3,2,1,0:T(2,128)} %param.6) | copy-start | bytes 393220
  9.2 53.5 %all-to-all-start = ((bf16[4,16,1,4096]{3,1,2,0:T(8,128)(2,1)}), bf16[4,16,1,4096]{3,1,2,0:T(8,128)(2,1)S(1)}, u32[]{:S(2)}, u32[]{:S(2)}) async-start(bf16[4,16,1,4096]{3,1,2,0:T(8,128)(2,1)} %pad_maximum_fusion), calls=%async_computation | async-start | bytes 1048576 | tf_op jit(solution)/shard_map/all_to_all | solution.py:110
  18.5 121.8 %reduce-scatter.4.cloned.1.call-start = ((), (), s32[]{:S(2)}) async-start(), calls=%async_computation.4 | async-start | bytes 6291456 | tf_op jit(solution)/shard_map/reduce_scatter | solution.py:155
  75.3 2.1 copy-start.11
  75.3 2.1 copy-start.12
  76.0 1.5 copy-start.17
  76.0 1.5 copy-start.18
  78.2 1.9 copy-start.9
  80.2 2.0 copy-start.15
  80.2 2.0 copy-start.16
  85.3 2.0 copy-start.13
  85.3 2.0 copy-start.14
  92.1 7.5 %copy-start.4 = (f32[1,16,1,4096]{3,1,2,0:T(8,128)S(1)}, f32[1,16,1,4096]{3,1,2,0:T(8,128)}, u32[]{:S(2)}) copy-start(f32[1,16,1,4096]{3,1,2,0:T(8,128)} %get-tuple-element.89) | copy-start | bytes 786436
  92.1 9.4 %copy-start.3 = (f32[1,16,1,4096]{3,1,2,0:T(8,128)S(1)}, f32[1,16,1,4096]{3,1,2,0:T(8,128)}, u32[]{:S(2)}) copy-start(f32[1,16,1,4096]{3,1,2,0:T(8,128)} %get-tuple-element.88) | copy-start | bytes 786436
  95.0 12.3 %copy-start.5 = (f32[8,8,2,32]{3,2,1,0:T(2,128)S(1)}, f32[8,8,2,32]{3,2,1,0:T(2,128)}, u32[]{:S(2)}) copy-start(f32[8,8,2,32]{3,2,1,0:T(2,128)} %mul.2738) | copy-start | bytes 49156
  107.2 4.6 %copy-start = (f32[16,1,8,8,2,32]{5,4,3,2,0,1:T(2,128)S(1)}, f32[16,1,8,8,2,32]{5,4,3,2,0,1:T(2,128)}, u32[]{:S(2)}) copy-start(f32[16,1,8,8,2,32]{5,4,3,2,0,1:T(2,128)} %squeeze.33) | copy-start | bytes 786436
  107.2 4.6 %copy-start.2 = (f32[16,1,8,8,2,32]{5,4,3,2,0,1:T(2,128)S(1)}, f32[16,1,8,8,2,32]{5,4,3,2,0,1:T(2,128)}, u32[]{:S(2)}) copy-start(f32[16,1,8,8,2,32]{5,4,3,2,0,1:T(2,128)} %squeeze.32) | copy-start | bytes 786436
  107.2 4.7 %copy-start.6 = (f32[8,8,2,32]{3,2,1,0:T(2,128)S(1)}, f32[8,8,2,32]{3,2,1,0:T(2,128)}, u32[]{:S(2)}) copy-start(f32[8,8,2,32]{3,2,1,0:T(2,128)} %mul.2752) | copy-start | bytes 49156
  107.2 4.7 %copy-start.8 = (f32[8,8,2,32]{3,2,1,0:T(2,128)S(1)}, f32[8,8,2,32]{3,2,1,0:T(2,128)}, u32[]{:S(2)}) copy-start(f32[8,8,2,32]{3,2,1,0:T(2,128)} %mul.2749) | copy-start | bytes 49156
  107.2 5.4 %copy-start.1 = (f32[16,1,8,8,2,32]{5,4,3,2,0,1:T(2,128)S(1)}, f32[16,1,8,8,2,32]{5,4,3,2,0,1:T(2,128)}, u32[]{:S(2)}) copy-start(f32[16,1,8,8,2,32]{5,4,3,2,0,1:T(2,128)} %squeeze.34) | copy-start | bytes 786436
  107.3 5.4 %copy-start.7 = (f32[8,8,2,32]{3,2,1,0:T(2,128)S(1)}, f32[8,8,2,32]{3,2,1,0:T(2,128)}, u32[]{:S(2)}) copy-start(f32[8,8,2,32]{3,2,1,0:T(2,128)} %mul.2756) | copy-start | bytes 49156
  120.1 70.4 %reduce-scatter.6.cloned.1.call-start = ((), (), s32[]{:S(2)}) async-start(), calls=%async_computation.5 | async-start | bytes 2359296 | tf_op jit(solution)/shard_map/reduce_scatter | solution.py:156
  140.3 90.2 %reduce-scatter.8.cloned.1.call-start = ((), (), s32[]{:S(2)}) async-start(), calls=%async_computation.6 | async-start | bytes 294912 | tf_op jit(solution)/shard_map/reduce_scatter | solution.py:157
Sparse Core Ops, SparseCore 0:
  120.2 20.0 reduce-scatter.3
  143.4 47.0 reduce-scatter.5
  193.5 36.9 reduce-scatter.7
